TPU v7x, 32 devices: a whole 2x2x4 slice. The times are simulated.
32 devices in a mesh: dp: 4 (over x, core), context: 8 (over z, y).
Axes of the slice: x: 2, y: 2, z: 4, core: 2. Of those that a mesh axis runs over, the one named last changes fastest.
Arguments:
- signal: bfloat16 [8192, 2048], P('context', 'dp'), may hold values from -6 to 6
- gating: bfloat16 [8192, 2048], P('context', 'dp'), may hold values from -6 to 6
- writer: bfloat16 [8192, 128], P('context'), may hold values from -2 to 2
- reader: bfloat16 [8192, 128], P('context'), may hold values from -2 to 2
- step_raw: float32 [8192, 32], P('context', 'dp'), may hold values from -7 to -1
- decay_log: float32 [32], P('dp'), may hold values from -12 to 1
- skip_gain: float32 [32], P('dp'), may hold values from 0.5 to 2
- norm_gain: float32 [2048], P('dp'), may hold values from 0.25 to 1.75
- cotangent: bfloat16 [8192, 2048], P('context', 'dp'), may hold values from -6 to 6
Outputs:
- grad_signal: bfloat16 [8192, 2048], P('context', 'dp')
- grad_gating: bfloat16 [8192, 2048], P('context', 'dp')
- grad_bc: float32 [8192, 256], P('context', 'dp')
- grad_step: float32 [8192, 32], P('context', 'dp')
All inputs are finite; a program needn't handle non-finite values.
Results may differ from a plain program's by a relative error of at most 0.0011.
Values sent between devices are 32-bit elements; how exact they have to be, the bound alone decides.
No kernel may reach another device: no remote copies, remote signals or barrier semaphores. Data moves between devices by JAX's collectives and lax.ppermute only.
A program may use at most 64 MiB of HBM per device.

v0:
```python
from functools import partial
import jax
import jax.numpy as jnp
from jax import lax
from jax.sharding import PartitionSpec as P

HEADS = 32
HEAD_DIM = 64
SPAN = 256
highest = lax.Precision.HIGHEST
epsilon = 1e-05


def block_step(state, pieces, decay_rate, skip_gain):
    signal_block, writer_block, reader_block, raw_block = pieces
    step_size = jax.nn.softplus(raw_block)
    log_decay = step_size * decay_rate[None, :]
    running = jnp.cumsum(log_decay, axis=0)
    length = raw_block.shape[0]
    causal = jnp.arange(length)[:, None] >= jnp.arange(length)[None, :]
    log_gaps = running[:, None, :] - running[None, :, :]
    decays = jnp.exp(jnp.where(causal[:, :, None], log_gaps, -jnp.inf))
    scores = jnp.dot(
        reader_block, writer_block.T, precision=highest, preferred_element_type=jnp.float32
    )
    mixing = scores[:, :, None] * decays * step_size[None, :, :]
    within = jnp.einsum("tsh,shp->thp", mixing, signal_block, precision=highest)
    across = jnp.exp(running)[:, :, None] * jnp.einsum(
        "tn,hpn->thp", reader_block, state, precision=highest
    )
    result = within + across + skip_gain[None, :, None] * signal_block
    weights = jnp.exp(running[-1][None, :] - running) * step_size
    new_state = jnp.exp(running[-1])[:, None, None] * state + jnp.einsum(
        "sh,shp,sn->hpn", weights, signal_block, writer_block, precision=highest
    )
    return (new_state, result)


def recurrence(signal, writer, reader, step_raw, start_state, decay_rate, skip_gain):
    tokens, head_count = step_raw.shape
    blocks = tokens // SPAN
    pieces = (
        signal.reshape(blocks, SPAN, head_count, HEAD_DIM),
        writer.reshape(blocks, SPAN, -1),
        reader.reshape(blocks, SPAN, -1),
        step_raw.reshape(blocks, SPAN, head_count),
    )
    advance = jax.checkpoint(partial(block_step, decay_rate=decay_rate, skip_gain=skip_gain))
    end_state, outputs = lax.scan(advance, start_state, pieces)
    return (outputs.reshape(tokens, head_count * HEAD_DIM), end_state)


def on_device(signal, gating, writer, reader, step_raw, decay_log, skip_gain, norm_gain, cotangent):
    tokens, head_count = step_raw.shape
    decay_rate = -jnp.exp(decay_log)
    signal_f = signal.astype(jnp.float32)
    writer_f = writer.astype(jnp.float32)
    reader_f = reader.astype(jnp.float32)
    step_size = jax.nn.softplus(step_raw)
    running = jnp.cumsum(step_size * decay_rate[None, :], axis=0)
    totals = running[-1]
    weights = jnp.exp(totals[None, :] - running) * step_size
    local_end = jnp.einsum(
        "sh,shp,sn->hpn",
        weights,
        signal_f.reshape(tokens, head_count, HEAD_DIM),
        writer_f,
        precision=highest,
    )
    all_totals = lax.all_gather(totals[None, :], "context", axis=0, tiled=True)
    inclusive = jnp.cumsum(all_totals, axis=0)
    exclusive = inclusive - all_totals
    position = lax.axis_index("context")
    devices = all_totals.shape[0]
    mine = (jnp.arange(devices) == position).astype(jnp.float32)
    inclusive_mine = jnp.dot(mine, inclusive, precision=highest, preferred_element_type=jnp.float32)
    exclusive_mine = jnp.dot(mine, exclusive, precision=highest, preferred_element_type=jnp.float32)
    pieces = lax.all_gather(local_end[None], "context", axis=0, tiled=True)
    indices = jnp.arange(pieces.shape[0])
    select = (indices[:, None] == jnp.arange(devices)[None, :]).astype(jnp.float32)
    inclusive_from = jnp.dot(
        select, inclusive, precision=highest, preferred_element_type=jnp.float32
    )
    factors = jnp.where(
        (indices < position)[:, None],
        jnp.exp(jnp.minimum(exclusive_mine[None, :] - inclusive_from, 0.0)),
        0.0,
    )
    incoming = jnp.einsum("fh,fhpn->hpn", factors, pieces, precision=highest)

    def local_pass(signal_in, writer_in, reader_in, raw_in, state_in):
        return recurrence(signal_in, writer_in, reader_in, raw_in, state_in, decay_rate, skip_gain)

    primal_out, pullback = jax.vjp(local_pass, signal_f, writer_f, reader_f, step_raw, incoming)
    output = primal_out[0]
    gating_f = gating.astype(jnp.float32)
    cotangent_f = cotangent.astype(jnp.float32)
    sigmoid = jax.nn.sigmoid(gating_f)
    activation = gating_f * sigmoid
    gated_output = output * activation
    weighted = norm_gain[None, :] * cotangent_f
    statistics = lax.psum(
        (jnp.sum(gated_output * gated_output, axis=1), jnp.sum(weighted * gated_output, axis=1)),
        "dp",
    )
    full_width = HEADS * HEAD_DIM
    scaling = lax.rsqrt(statistics[0] / full_width + epsilon)
    grad_gated = (
        weighted * scaling[:, None]
        - gated_output * (scaling * scaling * scaling * statistics[1] / full_width)[:, None]
    )
    grad_output = grad_gated * activation
    grad_gating = grad_gated * output * sigmoid * (1.0 + gating_f * (1.0 - sigmoid))
    influence = jnp.einsum(
        "th,thp,tn->hpn",
        jnp.exp(running),
        grad_output.reshape(tokens, head_count, HEAD_DIM),
        reader_f,
        precision=highest,
    )
    pieces = lax.all_gather(influence[None], "context", axis=0, tiled=True)
    indices = jnp.arange(pieces.shape[0])
    select = (indices[:, None] == jnp.arange(devices)[None, :]).astype(jnp.float32)
    exclusive_from = jnp.dot(
        select, exclusive, precision=highest, preferred_element_type=jnp.float32
    )
    factors = jnp.where(
        (indices > position)[:, None],
        jnp.exp(jnp.minimum(exclusive_from - inclusive_mine[None, :], 0.0)),
        0.0,
    )
    later_grad = jnp.einsum("fh,fhpn->hpn", factors, pieces, precision=highest)
    gradients = pullback((grad_output, later_grad))
    grad_signal = gradients[0]
    grad_writer = gradients[1]
    grad_reader = gradients[2]
    grad_step = gradients[3]
    grad_bc = lax.psum_scatter(
        jnp.concatenate([grad_writer, grad_reader], axis=1), "dp", scatter_dimension=1, tiled=True
    )
    return (grad_signal.astype(jnp.bfloat16), grad_gating.astype(jnp.bfloat16), grad_bc, grad_step)


def solution(mesh):
    in_specs = (
        P("context", "dp"),
        P("context", "dp"),
        P("context", None),
        P("context", None),
        P("context", "dp"),
        P("dp"),
        P("dp"),
        P("dp"),
        P("context", "dp"),
    )
    out_specs = (P("context", "dp"), P("context", "dp"), P("context", "dp"), P("context", "dp"))
    return jax.shard_map(
        on_device, mesh=mesh, in_specs=in_specs, out_specs=out_specs, check_vma=False
    )
```

profile of v0, /device:TPU:0, one launch (start us, length us, event | category | flops | bytes accessed | tf_op | source)
XLA Modules:
  0.0 398.9 jit_solution(4576556629796148414)
XLA Ops:
  9.3 2.3 reduce-window.68
  18.4 22.6 %all-gather.2 = f32[8,1,8]{2,1,0:T(1,128)S(1)} all-gather(f32[1,1,8]{2,1,0:T(1,128)S(1)} %bitcast.366), channel_id=1, replica_groups=mesh['dp'=4,'context'=8] {'context'}, dimensions={0}, use_global_device_ids=true | all-gather | bytes 288 | tf_op jit(solution)/shard_map/all_gather | solution.py:70
  47.6 21.7 %all-gather.6.cloned.1.call-done = f32[64,64,128]{2,1,0:T(8,128)} async-done(((f32[8,64,128]{2,1,0:T(8,128)}), f32[64,64,128]{2,1,0:T(8,128)}) %all-gather.6.cloned.1.call-update) | async-done | bytes 2097168 | tf_op jit(solution)/shard_map/all_gather | solution.py:78
  69.4 4.4 %fusion.102 = f32[8,1,64,128]{3,1,2,0:T(1,128)S(1)} fusion(f32[8,8,1,1]{0,2,3,1:T(1,128)S(1)} %copy.85, f32[8,8,64,128]{3,2,1,0:T(8,128)} %bitcast.349), kind=kOutput, calls=%fused_computation.142 | convolution fusion | flops 6291456 | bytes 2359552 | tf_op jit(solution)/shard_map/fh,fhpn->hpn/dot_general | solution.py:89
  73.8 92.1 %while.39 = (s32[]{:T(128)}, f32[8,64,128]{2,1,0:T(8,128)S(1)}, f32[4,256,8,64]{1,0,3,2:T(4,128)}, f32[4,8,64,128]{3,2,1,0:T(8,128)}, f32[4,256,8]{1,2,0:T(8,128...) while((s32[]{:T(128)}, f32[8,64,128]{2,1,0:T(8,128)S(1)}, ...), condition=%wide.region_6.7_spmd.clone, body=%wide.region_3.6_spmd.clone.sunk | while | flops 909158400 | bytes 7812925 | solution.py:49
  76.1 3.5 fusion.231
  81.8 12.3 %dynamic_update_slice.68 = f32[4,256,8,64]{1,0,3,2:T(4,128)} dynamic-update-slice(f32[4,256,8,64]{1,0,3,2:T(4,128)} %get-tuple-element.828, f32[1,256,8,64]{1,0,3,2:T(1,128)S(1)} %copy.123, s32[]{:T(128)} %get-tuple-element.826, s32[]{:T(128)} %constant.134.clone.1..sunk, s32[]{:T(128)} %constant.134.clone.1..sunk, s32[]{:T(128)} %constant.134.clone.1..sunk) | dynamic-update-slice | bytes 1048580 | tf_op jit(solution)/shard_map/jvp()/while/body/jit(dynamic_update_index_in_dim)/dynamic_update_slice | solution.py:49
  99.1 3.5 fusion.231
  104.8 12.3 %dynamic_update_slice.68 = f32[4,256,8,64]{1,0,3,2:T(4,128)} dynamic-update-slice(f32[4,256,8,64]{1,0,3,2:T(4,128)} %get-tuple-element.828, f32[1,256,8,64]{1,0,3,2:T(1,128)S(1)} %copy.123, s32[]{:T(128)} %get-tuple-element.826, s32[]{:T(128)} %constant.134.clone.1..sunk, s32[]{:T(128)} %constant.134.clone.1..sunk, s32[]{:T(128)} %constant.134.clone.1..sunk) | dynamic-update-slice | bytes 1048580 | tf_op jit(solution)/shard_map/jvp()/while/body/jit(dynamic_update_index_in_dim)/dynamic_update_slice | solution.py:49
  122.1 3.5 fusion.231
  127.9 12.3 %dynamic_update_slice.68 = f32[4,256,8,64]{1,0,3,2:T(4,128)} dynamic-update-slice(f32[4,256,8,64]{1,0,3,2:T(4,128)} %get-tuple-element.828, f32[1,256,8,64]{1,0,3,2:T(1,128)S(1)} %copy.123, s32[]{:T(128)} %get-tuple-element.826, s32[]{:T(128)} %constant.134.clone.1..sunk, s32[]{:T(128)} %constant.134.clone.1..sunk, s32[]{:T(128)} %constant.134.clone.1..sunk) | dynamic-update-slice | bytes 1048580 | tf_op jit(solution)/shard_map/jvp()/while/body/jit(dynamic_update_index_in_dim)/dynamic_update_slice | solution.py:49
  145.2 3.5 fusion.231
  150.9 12.3 %dynamic_update_slice.68 = f32[4,256,8,64]{1,0,3,2:T(4,128)} dynamic-update-slice(f32[4,256,8,64]{1,0,3,2:T(4,128)} %get-tuple-element.828, f32[1,256,8,64]{1,0,3,2:T(1,128)S(1)} %copy.123, s32[]{:T(128)} %get-tuple-element.826, s32[]{:T(128)} %constant.134.clone.1..sunk, s32[]{:T(128)} %constant.134.clone.1..sunk, s32[]{:T(128)} %constant.134.clone.1..sunk) | dynamic-update-slice | bytes 1048580 | tf_op jit(solution)/shard_map/jvp()/while/body/jit(dynamic_update_index_in_dim)/dynamic_update_slice | solution.py:49
  169.3 6.0 %all-reduce.2 = (f32[1024]{0:T(1024)S(1)}, f32[1024]{0:T(1024)S(1)}) all-reduce(f32[1024]{0:T(1024)S(1)} %get-tuple-element.523, f32[1024]{0:T(1024)S(1)} %get-tuple-element.522), channel_id=1, replica_groups=mesh['dp'=4,'context'=8] {'dp'}, use_global_device_ids=true, to_apply=%region_10.11 | all-reduce | flops 2048 | bytes 16384 | tf_op jit(solution)/shard_map/psum | solution.py:102
  175.3 4.6 %fusion.99 = (bf16[1024,512]{0,1:T(8,128)(2,1)}, f32[1024,512]{0,1:T(8,128)S(1)}) fusion(bf16[1024,512]{0,1:T(8,128)(2,1)} %copy-done.2, f32[1024,512]{0,1:T(8,128)} %bitcast.347, bf16[1024,512]{0,1:T(8,128)(2,1)} %copy-done.1, f32[1024]{0:T(1024)S(1)} %get-tuple-element.597, f32[1024]{0:T(1024)S(1)} %get-tuple-element.596, f32[512]{0:T(512)S(1)} %copy-done.16), kind=kLoop, calls=%fused_computation.139 | loop fusion | flops 9961472 | bytes 7350272 | tf_op jit(solution)/shard_map/convert_element_type | solution.py:141
  184.1 45.7 %all-gather.8.cloned.1.call-done = f32[64,64,128]{2,1,0:T(8,128)} async-done(((f32[8,64,128]{2,1,0:T(8,128)}), f32[64,64,128]{2,1,0:T(8,128)}) %all-gather.8.cloned.1.call-update) | async-done | bytes 2097168 | tf_op jit(solution)/shard_map/all_gather | solution.py:121
  229.8 4.4 %fusion.100 = f32[8,1,64,128]{3,1,2,0:T(1,128)S(1)} fusion(f32[8,8,1,1]{0,2,3,1:T(1,128)S(1)} %copy.88, f32[8,8,64,128]{3,2,1,0:T(8,128)} %bitcast.350), kind=kOutput, calls=%fused_computation.140 | convolution fusion | flops 6291456 | bytes 2359552 | tf_op jit(solution)/shard_map/fh,fhpn->hpn/dot_general | solution.py:132
  237.7 127.6 %while.38 = (s32[]{:T(128)}, f32[8,64,128]{2,1,0:T(8,128)S(1)}, bf16[4,256,8,64]{1,3,2,0:T(8,128)(2,1)}, f32[4,256,128]{2,1,0:T(8,128)}, f32[4,256,128]{2,1,0:T(...) while((s32[]{:T(128)}, f32[8,64,128]{2,1,0:T(8,128)S(1)}, ...), condition=%wide.region_23.24_spmd, body=%wide.region_11.23_spmd.sunk | while | flops 2125232128 | bytes 24865956 | solution.py:49
  247.7 4.0 %fusion.215 = (f32[256,8]{0,1:T(8,128)}, f32[256,8]{0,1:T(8,128)}, f32[256,8]{0,1:T(8,128)}, f32[256,256]{1,0:T(8,128)S(1)}) fusion(f32[256,8]{0,1:T(8,128)S(1)} %get-tuple-element.788, f32[256,8]{0,1:T(8,128)S(1)} %get-tuple-element.783, f32[256,256]{1,0:T(8,128)S(1)} %fusion.214, pred[256,256]{1,0:T(8,128)(4,1)S(1)} %iota_compare_fusion.8, ...), kind=kOutput, calls=%fused_computation.66.clone.1 | convolution fusion | flops 409397248 | bytes 1679360 | tf_op jit(solution)/shard_map/transpose(jvp())/while/body/eval_jaxpr/checkpoint/tsh,shp->thp/dot_general | solution.py:27
  253.8 3.1 reduce-window.80
  265.3 2.6 fusion.217
  269.6 2.1 constant_dynamic-slice_fusion.2
  279.6 4.0 %fusion.215 = (f32[256,8]{0,1:T(8,128)}, f32[256,8]{0,1:T(8,128)}, f32[256,8]{0,1:T(8,128)}, f32[256,256]{1,0:T(8,128)S(1)}) fusion(f32[256,8]{0,1:T(8,128)S(1)} %get-tuple-element.788, f32[256,8]{0,1:T(8,128)S(1)} %get-tuple-element.783, f32[256,256]{1,0:T(8,128)S(1)} %fusion.214, pred[256,256]{1,0:T(8,128)(4,1)S(1)} %iota_compare_fusion.8, ...), kind=kOutput, calls=%fused_computation.66.clone.1 | convolution fusion | flops 409397248 | bytes 1679360 | tf_op jit(solution)/shard_map/transpose(jvp())/while/body/eval_jaxpr/checkpoint/tsh,shp->thp/dot_general | solution.py:27
  285.7 3.1 reduce-window.80
  297.2 2.6 fusion.217
  311.5 4.0 %fusion.215 = (f32[256,8]{0,1:T(8,128)}, f32[256,8]{0,1:T(8,128)}, f32[256,8]{0,1:T(8,128)}, f32[256,256]{1,0:T(8,128)S(1)}) fusion(f32[256,8]{0,1:T(8,128)S(1)} %get-tuple-element.788, f32[256,8]{0,1:T(8,128)S(1)} %get-tuple-element.783, f32[256,256]{1,0:T(8,128)S(1)} %fusion.214, pred[256,256]{1,0:T(8,128)(4,1)S(1)} %iota_compare_fusion.8, ...), kind=kOutput, calls=%fused_computation.66.clone.1 | convolution fusion | flops 409397248 | bytes 1679360 | tf_op jit(solution)/shard_map/transpose(jvp())/while/body/eval_jaxpr/checkpoint/tsh,shp->thp/dot_general | solution.py:27
  317.6 3.1 reduce-window.80
  329.1 2.6 fusion.217
  343.4 4.0 %fusion.215 = (f32[256,8]{0,1:T(8,128)}, f32[256,8]{0,1:T(8,128)}, f32[256,8]{0,1:T(8,128)}, f32[256,256]{1,0:T(8,128)S(1)}) fusion(f32[256,8]{0,1:T(8,128)S(1)} %get-tuple-element.788, f32[256,8]{0,1:T(8,128)S(1)} %get-tuple-element.783, f32[256,256]{1,0:T(8,128)S(1)} %fusion.214, pred[256,256]{1,0:T(8,128)(4,1)S(1)} %iota_compare_fusion.8, ...), kind=kOutput, calls=%fused_computation.66.clone.1 | convolution fusion | flops 409397248 | bytes 1679360 | tf_op jit(solution)/shard_map/transpose(jvp())/while/body/eval_jaxpr/checkpoint/tsh,shp->thp/dot_general | solution.py:27
  349.5 3.1 reduce-window.80
  361.0 2.6 fusion.217
  373.6 18.8 %reduce-scatter.2.cloned.1.call-done = f32[1024,64]{0,1:T(8,128)} async-done(((f32[1024,256]{0,1:T(8,128)}), f32[1024,64]{0,1:T(8,128)}) %reduce-scatter.2.cloned.1.call-update) | async-done | bytes 262160 | tf_op jit(solution)/shard_map/reduce_scatter | solution.py:138
  (303 shorter events, 149.1 us)
Async XLA Ops:
  7.2 62.2 %all-gather.6.cloned.1.call-start = ((), (), s32[]{:S(2)}) async-start(), calls=%async_computation.2 | async-start | bytes 2359296 | tf_op jit(solution)/shard_map/all_gather | solution.py:78
  17.3 212.5 %all-gather.8.cloned.1.call-start = ((), (), s32[]{:S(2)}) async-start(), calls=%async_computation.3 | async-start | bytes 2359296 | tf_op jit(solution)/shard_map/all_gather | solution.py:121
  41.3 1.8 copy-start.10
  43.0 1.4 copy-start.8
  45.0 123.0 %copy-start.1 = (bf16[1024,512]{0,1:T(8,128)(2,1)}, bf16[1024,512]{0,1:T(8,128)(2,1)S(1)}, u32[]{:S(2)}) copy-start(bf16[1024,512]{0,1:T(8,128)(2,1)S(1)} %copy.69) | copy-start | bytes 3145732
  45.0 28.8 %copy-start.7 = (f32[1024,8]{0,1:T(8,128)S(1)}, f32[1024,8]{0,1:T(8,128)}, u32[]{:S(2)}) copy-start(f32[1024,8]{0,1:T(8,128)} %param.17) | copy-start | bytes 98308
  46.9 121.1 %copy-start.2 = (bf16[1024,512]{0,1:T(8,128)(2,1)}, bf16[1024,512]{0,1:T(8,128)(2,1)S(1)}, u32[]{:S(2)}) copy-start(bf16[1024,512]{0,1:T(8,128)(2,1)S(1)} %copy.73) | copy-start | bytes 3145732
  165.9 2.1 copy-start.16
  168.0 1.3 copy-start
  175.3 4.6 %copy-start.11 = (bf16[1024,128]{1,0:T(8,128)(2,1)S(1)}, bf16[1024,128]{1,0:T(8,128)(2,1)}, u32[]{:S(2)}) copy-start(bf16[1024,128]{1,0:T(8,128)(2,1)} %param.16) | copy-start | bytes 786436
  181.8 210.6 %reduce-scatter.2.cloned.1.call-start = ((), (), s32[]{:S(2)}) async-start(), calls=%async_computation.1 | async-start | bytes 1310720 | tf_op jit(solution)/shard_map/reduce_scatter | solution.py:138
  247.6 4.1 %copy-start.14 = (f32[256,8]{0,1:T(8,128)}, f32[256,8]{0,1:T(8,128)S(1)}, u32[]{:S(2)}) copy-start(f32[256,8]{0,1:T(8,128)S(1)} %get-tuple-element.788) | copy-start | bytes 24580 | tf_op jit(solution)/shard_map/transpose(jvp())/while
  258.8 6.4 %copy-start.4 = (bf16[4,256,8,64]{1,3,2,0:T(8,128)(2,1)S(1)}, bf16[4,256,8,64]{1,3,2,0:T(8,128)(2,1)}, u32[]{:S(2)}) copy-start(bf16[4,256,8,64]{1,3,2,0:T(8,128)(2,1)} %get-tuple-element.873) | copy-start | bytes 3145732 | tf_op jit(solution)/shard_map/transpose(jvp())/while
  258.8 6.4 %copy-start.15 = (f32[256,8]{0,1:T(8,128)S(1)}, f32[256,8]{0,1:T(8,128)}, u32[]{:S(2)}) copy-start(f32[256,8]{0,1:T(8,128)} %copy-done.14) | copy-start | bytes 24580 | tf_op jit(solution)/shard_map/transpose(jvp())/while
  265.3 3.6 copy-start.13
  267.9 1.0 copy-start.5
  279.5 4.1 %copy-start.14 = (f32[256,8]{0,1:T(8,128)}, f32[256,8]{0,1:T(8,128)S(1)}, u32[]{:S(2)}) copy-start(f32[256,8]{0,1:T(8,128)S(1)} %get-tuple-element.788) | copy-start | bytes 24580 | tf_op jit(solution)/shard_map/transpose(jvp())/while
  290.7 6.5 %copy-start.4 = (bf16[4,256,8,64]{1,3,2,0:T(8,128)(2,1)S(1)}, bf16[4,256,8,64]{1,3,2,0:T(8,128)(2,1)}, u32[]{:S(2)}) copy-start(bf16[4,256,8,64]{1,3,2,0:T(8,128)(2,1)} %get-tuple-element.873) | copy-start | bytes 3145732 | tf_op jit(solution)/shard_map/transpose(jvp())/while
  290.7 6.5 %copy-start.15 = (f32[256,8]{0,1:T(8,128)S(1)}, f32[256,8]{0,1:T(8,128)}, u32[]{:S(2)}) copy-start(f32[256,8]{0,1:T(8,128)} %copy-done.14) | copy-start | bytes 24580 | tf_op jit(solution)/shard_map/transpose(jvp())/while
  297.2 3.6 copy-start.13
  299.8 1.0 copy-start.5
  311.5 4.1 %copy-start.14 = (f32[256,8]{0,1:T(8,128)}, f32[256,8]{0,1:T(8,128)S(1)}, u32[]{:S(2)}) copy-start(f32[256,8]{0,1:T(8,128)S(1)} %get-tuple-element.788) | copy-start | bytes 24580 | tf_op jit(solution)/shard_map/transpose(jvp())/while
  322.7 6.4 %copy-start.4 = (bf16[4,256,8,64]{1,3,2,0:T(8,128)(2,1)S(1)}, bf16[4,256,8,64]{1,3,2,0:T(8,128)(2,1)}, u32[]{:S(2)}) copy-start(bf16[4,256,8,64]{1,3,2,0:T(8,128)(2,1)} %get-tuple-element.873) | copy-start | bytes 3145732 | tf_op jit(solution)/shard_map/transpose(jvp())/while
  322.7 6.4 %copy-start.15 = (f32[256,8]{0,1:T(8,128)S(1)}, f32[256,8]{0,1:T(8,128)}, u32[]{:S(2)}) copy-start(f32[256,8]{0,1:T(8,128)} %copy-done.14) | copy-start | bytes 24580 | tf_op jit(solution)/shard_map/transpose(jvp())/while
  329.1 3.6 copy-start.13
  331.7 1.0 copy-start.5
  343.4 4.1 %copy-start.14 = (f32[256,8]{0,1:T(8,128)}, f32[256,8]{0,1:T(8,128)S(1)}, u32[]{:S(2)}) copy-start(f32[256,8]{0,1:T(8,128)S(1)} %get-tuple-element.788) | copy-start | bytes 24580 | tf_op jit(solution)/shard_map/transpose(jvp())/while
  354.6 6.4 %copy-start.4 = (bf16[4,256,8,64]{1,3,2,0:T(8,128)(2,1)S(1)}, bf16[4,256,8,64]{1,3,2,0:T(8,128)(2,1)}, u32[]{:S(2)}) copy-start(bf16[4,256,8,64]{1,3,2,0:T(8,128)(2,1)} %get-tuple-element.873) | copy-start | bytes 3145732 | tf_op jit(solution)/shard_map/transpose(jvp())/while
  354.6 6.4 %copy-start.15 = (f32[256,8]{0,1:T(8,128)S(1)}, f32[256,8]{0,1:T(8,128)}, u32[]{:S(2)}) copy-start(f32[256,8]{0,1:T(8,128)} %copy-done.14) | copy-start | bytes 24580 | tf_op jit(solution)/shard_map/transpose(jvp())/while
  361.0 3.6 copy-start.13
  366.5 2.4 copy-start.3
  368.9 1.4 copy-start.6
  (6 other events, 4.2 us)
Sparse Core Ops, SparseCore 0:
  17.4 51.8 all-gather.5
  181.9 47.9 all-gather.7
  369.1 23.2 reduce-scatter.1
where the time goes:
time: 402 us; the launch traced here: 399 us
  local copies, waits for them, and re-layouts  115 us (29%)
  matrix products  98.3 us (24%)
  waiting for transfers between devices  86.3 us (21%)
  other arithmetic  56.4 us (14%)
  blocking collectives  28.5 us (7%)
  between operations  14 us (3%)
    dynamic_update_slice x12, local copies, waits for them, and re-layouts, recurrence(): end_state, outputs = lax.scan(advance, start_state, pieces)  54.4 us
    all_gather x1, waiting for transfers between devices, on_device(): pieces = lax.all_gather(influence[None], 'context', axis=0, tiled=True)  45.7 us
    dot_general x12, matrix products, block_step(): within = jnp.einsum('tsh,shp->thp', mixing, signal_block, precision=highest)  40.6 us
    another operation x40, other arithmetic  34.5 us
    all_gather x1, blocking collectives, on_device(): all_totals = lax.all_gather(totals[None, :], 'context', axis=0, tiled=True)  22.6 us
    all_gather x1, waiting for transfers between devices, on_device(): pieces = lax.all_gather(local_end[None], 'context', axis=0, tiled=True)  21.7 us
    reduce_scatter x1, waiting for transfers between devices, on_device(): lax.psum_scatter(jnp.concatenate([grad_writer, grad_reader], axis=1), 'dp...  18.8 us
    dot_general x16, matrix products, block_step(): jnp.dot(reader_block, writer_block.T, precision=highest, preferred_elemen...  15.9 us
  transfers between devices with their start and end apart: 3, of which 3 were waited for; matrix products, arithmetic and copies ran while one was open for 3% of the time, Pallas kernels for 0%

commit v1 on v0

--- a/solution.py
+++ b/solution.py
@@ -9,6 +9,13 @@
 SPAN = 256
 highest = lax.Precision.HIGHEST
 epsilon = 1e-05
+
+
+def _serve_classes(field, where_dim):
+    before = list(field.shape[1:])
+    before[where_dim] *= field.shape[0]
+    built = jnp.moveaxis(field, 0, where_dim).reshape(before)
+    return built
 
 
 def block_step(state, pieces, decay_rate, skip_gain):
@@ -75,7 +82,32 @@
     mine = (jnp.arange(devices) == position).astype(jnp.float32)
     inclusive_mine = jnp.dot(mine, inclusive, precision=highest, preferred_element_type=jnp.float32)
     exclusive_mine = jnp.dot(mine, exclusive, precision=highest, preferred_element_type=jnp.float32)
-    pieces = lax.all_gather(local_end[None], "context", axis=0, tiled=True)
+
+    def digits_tell(in_array, mesh_dim, d0):
+        nodes = lax.axis_size(mesh_dim)
+        response = range(nodes)
+        block_out = map(lambda ix: (ix, (ix + 1) % nodes), response)
+        sheets = list(block_out)
+        entries = [(jj, no) for no, jj in sheets]
+        block_last, r2 = ([], [])
+        for i0 in range(nodes - 1):
+            if i0 % 2 == 0:
+                val2 = lax.ppermute(
+                    block_last[-1] if block_last else in_array, axis_name=mesh_dim, perm=sheets
+                )
+                block_last.append(val2)
+            else:
+                all_rows = lax.ppermute(r2[-1] if r2 else in_array, mesh_dim, perm=entries)
+                r2.append(all_rows)
+        d_next = jnp.stack([*block_last[::-1], in_array, *r2])
+        w_next = len(block_last)
+        t_next = lax.axis_index(mesh_dim)
+        reply = t_next - w_next
+        d_next = d_next[(jnp.arange(nodes) - reply) % nodes]
+        arr_out = _serve_classes(d_next, d0)
+        return arr_out
+
+    pieces = digits_tell(local_end[None], mesh_dim="context", d0=0)
     indices = jnp.arange(pieces.shape[0])
     select = (indices[:, None] == jnp.arange(devices)[None, :]).astype(jnp.float32)
     inclusive_from = jnp.dot(

time: 402 us -> 418 us (1.040)
  starting transfers between devices: 0.12 us -> 15.4 us
  local copies, waits for them, and re-layouts: 115 us -> 127 us
  waiting for transfers between devices: 86.3 us -> 78.7 us
    all_gather x1 -> x0, waiting for transfers between devices: 21.7 us -> none  [on_device(): pieces = lax.all_gather(local_end[None], 'context', axis=0, tiled=True)]
    ppermute x0 -> x7, waiting for transfers between devices: none -> 15.5 us  [the longest x4 15.5 us: digits_tell(): lax.ppermute(block_last[-1] if block_last else in_array, axis_name=mesh_d...]
    ppermute x0 -> x7, starting transfers between devices: none -> 15.3 us  [the longest x3 8.02 us: digits_tell(): all_rows = lax.ppermute(r2[-1] if r2 else in_array, mesh_dim, perm=entries)]
    unnamed x31 -> x50, local copies, waits for them, and re-layouts: 13.8 us -> 22.7 us
    another operation x29 -> x30, local copies, waits for them, and re-layouts: 9.94 us -> 10.7 us
  transfers between devices with their start and end apart: 3 -> 9, of which waited for: 3 -> 4; matrix products, arithmetic and copies ran while one was open for 3% -> 6% of each run, Pallas kernels for 0% -> 0%
where the time goes in v1:
time: 418 us; the launch traced here: 415 us
  local copies, waits for them, and re-layouts  127 us (30%)
  matrix products  97.4 us (23%)
  waiting for transfers between devices  78.7 us (19%)
  other arithmetic  56.4 us (13%)
  blocking collectives  24.5 us (6%)
  starting transfers between devices  15.4 us (4%)
  between operations  14.4 us (3%)
    dynamic_update_slice x12, local copies, waits for them, and re-layouts, recurrence(): end_state, outputs = lax.scan(advance, start_state, pieces)  54.4 us
    all_gather x1, waiting for transfers between devices, on_device(): pieces = lax.all_gather(influence[None], 'context', axis=0, tiled=True)  44.3 us
    dot_general x12, matrix products, block_step(): within = jnp.einsum('tsh,shp->thp', mixing, signal_block, precision=highest)  40.5 us
    another operation x40, other arithmetic  34.5 us
    unnamed x50, local copies, waits for them, and re-layouts  22.7 us
    reduce_scatter x1, waiting for transfers between devices, on_device(): lax.psum_scatter(jnp.concatenate([grad_writer, grad_reader], axis=1), 'dp...  18.8 us
    all_gather x1, blocking collectives, on_device(): all_totals = lax.all_gather(totals[None, :], 'context', axis=0, tiled=True)  18.5 us
    dot_general x16, matrix products, block_step(): jnp.dot(reader_block, writer_block.T, precision=highest, preferred_elemen...  15.8 us
  transfers between devices with their start and end apart: 9, of which 4 were waited for; matrix products, arithmetic and copies ran while one was open for 6% of the time, Pallas kernels for 0%

profile of v1, /device:TPU:0, one launch (start us, length us, event | category | flops | bytes accessed | tf_op | source)
XLA Modules:
  0.0 414.9 jit_solution(5489252964611087798)
XLA Ops:
  16.6 3.0 collective-permute-start
  19.6 9.3 %collective-permute-done = f32[1,8,64,128]{3,2,1,0:T(8,128)S(1)} collective-permute-done((f32[1,8,64,128]{3,2,1,0:T(8,128)S(1)}, f32[1,8,64,128]{3,2,1,0:T(8,128)S(1)}, u32[]{:S(2)}, u32[]{:S(2)}) %collective-permute-start) | collective-permute-done | bytes 262176 | tf_op jit(solution)/shard_map/ppermute | solution.py:95
  29.0 4.7 %collective-permute-start.4 = (f32[1,8,64,128]{3,2,1,0:T(8,128)S(1)}, f32[1,8,64,128]{3,2,1,0:T(8,128)}, u32[]{:S(2)}, u32[]{:S(2)}) collective-permute-start(f32[1,8,64,128]{3,2,1,0:T(8,128)S(1)} %bitcast.376), channel_id=1, source_target_pairs={{1,0},{2,1},{3,2},{4,3},{5,4},{6,5},{7,6},{0,7},{9,8},{10,9},{11,1... | collective-permute-start | bytes 786440 | tf_op jit(solution)/shard_map/ppermute | solution.py:100
  33.7 6.2 %collective-permute-done.1 = f32[1,8,64,128]{3,2,1,0:T(8,128)S(1)} collective-permute-done((f32[1,8,64,128]{3,2,1,0:T(8,128)S(1)}, f32[1,8,64,128]{3,2,1,0:T(8,128)S(1)}, u32[]{:S(2)}, u32[]{:S(2)}) %collective-permute-start.1) | collective-permute-done | bytes 262176 | tf_op jit(solution)/shard_map/ppermute | solution.py:95
  42.3 18.5 %all-gather.1 = f32[8,1,8]{2,1,0:T(1,128)S(1)} all-gather(f32[1,1,8]{2,1,0:T(1,128)S(1)} %bitcast.386), channel_id=1, replica_groups=mesh['dp'=4,'context'=8] {'context'}, dimensions={0}, use_global_device_ids=true | all-gather | bytes 288 | tf_op jit(solution)/shard_map/all_gather | solution.py:77
  70.7 3.0 collective-permute-start.6
  83.3 3.6 gather_fusion
  86.9 4.4 %fusion.102 = f32[8,1,64,128]{3,1,2,0:T(1,128)S(1)} fusion(f32[8,8,1,1]{0,2,3,1:T(1,128)S(1)} %copy.85, f32[8,8,64,128]{3,2,1,0:T(8,128)} %gather_fusion), kind=kOutput, calls=%fused_computation.143 | convolution fusion | flops 6291456 | bytes 2359552 | tf_op jit(solution)/shard_map/fh,fhpn->hpn/dot_general | solution.py:121
  91.3 92.1 %while.39 = (s32[]{:T(128)}, f32[8,64,128]{2,1,0:T(8,128)S(1)}, f32[4,256,8,64]{1,0,3,2:T(4,128)}, f32[4,8,64,128]{3,2,1,0:T(8,128)}, f32[4,256,8]{1,2,0:T(8,128...) while((s32[]{:T(128)}, f32[8,64,128]{2,1,0:T(8,128)S(1)}, ...), condition=%wide.region_6.7_spmd.clone, body=%wide.region_3.6_spmd.clone.sunk | while | flops 909158400 | bytes 7812925 | solution.py:56
  93.6 3.5 fusion.233
  99.3 12.3 %dynamic_update_slice.68 = f32[4,256,8,64]{1,0,3,2:T(4,128)} dynamic-update-slice(f32[4,256,8,64]{1,0,3,2:T(4,128)} %get-tuple-element.828, f32[1,256,8,64]{1,0,3,2:T(1,128)S(1)} %copy.123, s32[]{:T(128)} %get-tuple-element.826, s32[]{:T(128)} %constant.150.clone.1..sunk, s32[]{:T(128)} %constant.150.clone.1..sunk, s32[]{:T(128)} %constant.150.clone.1..sunk) | dynamic-update-slice | bytes 1048580 | tf_op jit(solution)/shard_map/jvp()/while/body/jit(dynamic_update_index_in_dim)/dynamic_update_slice | solution.py:56
  116.6 3.5 fusion.233
  122.4 12.3 %dynamic_update_slice.68 = f32[4,256,8,64]{1,0,3,2:T(4,128)} dynamic-update-slice(f32[4,256,8,64]{1,0,3,2:T(4,128)} %get-tuple-element.828, f32[1,256,8,64]{1,0,3,2:T(1,128)S(1)} %copy.123, s32[]{:T(128)} %get-tuple-element.826, s32[]{:T(128)} %constant.150.clone.1..sunk, s32[]{:T(128)} %constant.150.clone.1..sunk, s32[]{:T(128)} %constant.150.clone.1..sunk) | dynamic-update-slice | bytes 1048580 | tf_op jit(solution)/shard_map/jvp()/while/body/jit(dynamic_update_index_in_dim)/dynamic_update_slice | solution.py:56
  139.6 3.5 fusion.233
  145.4 12.3 %dynamic_update_slice.68 = f32[4,256,8,64]{1,0,3,2:T(4,128)} dynamic-update-slice(f32[4,256,8,64]{1,0,3,2:T(4,128)} %get-tuple-element.828, f32[1,256,8,64]{1,0,3,2:T(1,128)S(1)} %copy.123, s32[]{:T(128)} %get-tuple-element.826, s32[]{:T(128)} %constant.150.clone.1..sunk, s32[]{:T(128)} %constant.150.clone.1..sunk, s32[]{:T(128)} %constant.150.clone.1..sunk) | dynamic-update-slice | bytes 1048580 | tf_op jit(solution)/shard_map/jvp()/while/body/jit(dynamic_update_index_in_dim)/dynamic_update_slice | solution.py:56
  162.7 3.5 fusion.233
  168.4 12.3 %dynamic_update_slice.68 = f32[4,256,8,64]{1,0,3,2:T(4,128)} dynamic-update-slice(f32[4,256,8,64]{1,0,3,2:T(4,128)} %get-tuple-element.828, f32[1,256,8,64]{1,0,3,2:T(1,128)S(1)} %copy.123, s32[]{:T(128)} %get-tuple-element.826, s32[]{:T(128)} %constant.150.clone.1..sunk, s32[]{:T(128)} %constant.150.clone.1..sunk, s32[]{:T(128)} %constant.150.clone.1..sunk) | dynamic-update-slice | bytes 1048580 | tf_op jit(solution)/shard_map/jvp()/while/body/jit(dynamic_update_index_in_dim)/dynamic_update_slice | solution.py:56
  186.8 6.0 %all-reduce.2 = (f32[1024]{0:T(1024)S(1)}, f32[1024]{0:T(1024)S(1)}) all-reduce(f32[1024]{0:T(1024)S(1)} %get-tuple-element.523, f32[1024]{0:T(1024)S(1)} %get-tuple-element.522), channel_id=1, replica_groups=mesh['dp'=4,'context'=8] {'dp'}, use_global_device_ids=true, to_apply=%region_10.11 | all-reduce | flops 2048 | bytes 16384 | tf_op jit(solution)/shard_map/psum | solution.py:134
  192.8 4.6 %fusion.99 = (bf16[1024,512]{0,1:T(8,128)(2,1)}, f32[1024,512]{0,1:T(8,128)S(1)}) fusion(bf16[1024,512]{0,1:T(8,128)(2,1)} %copy-done.2, f32[1024,512]{0,1:T(8,128)} %bitcast.366, bf16[1024,512]{0,1:T(8,128)(2,1)} %copy-done.1, f32[1024]{0:T(1024)S(1)} %get-tuple-element.597, f32[1024]{0:T(1024)S(1)} %get-tuple-element.596, f32[512]{0:T(512)S(1)} %copy-done.22), kind=kLoop, calls=%fused_computation.140 | loop fusion | flops 9961472 | bytes 7350272 | tf_op jit(solution)/shard_map/convert_element_type | solution.py:173
  201.7 44.3 %all-gather.4.cloned.1.call-done = f32[64,64,128]{2,1,0:T(8,128)} async-done(((f32[8,64,128]{2,1,0:T(8,128)}), f32[64,64,128]{2,1,0:T(8,128)}) %all-gather.4.cloned.1.call-update) | async-done | bytes 2097168 | tf_op jit(solution)/shard_map/all_gather | solution.py:153
  246.0 4.4 %fusion.100 = f32[8,1,64,128]{3,1,2,0:T(1,128)S(1)} fusion(f32[8,8,1,1]{0,2,3,1:T(1,128)S(1)} %copy.88, f32[8,8,64,128]{3,2,1,0:T(8,128)} %bitcast.368), kind=kOutput, calls=%fused_computation.141 | convolution fusion | flops 6291456 | bytes 2359552 | tf_op jit(solution)/shard_map/fh,fhpn->hpn/dot_general | solution.py:164
  253.8 127.1 %while.38 = (s32[]{:T(128)}, f32[8,64,128]{2,1,0:T(8,128)S(1)}, bf16[4,256,8,64]{1,3,2,0:T(8,128)(2,1)}, f32[4,256,128]{2,1,0:T(8,128)}, f32[4,256,128]{2,1,0:T(...) while((s32[]{:T(128)}, f32[8,64,128]{2,1,0:T(8,128)S(1)}, ...), condition=%wide.region_23.24_spmd, body=%wide.region_11.23_spmd.sunk | while | flops 2125232128 | bytes 24865956 | solution.py:56
  263.7 4.0 fusion.217
  269.8 3.1 reduce-window.80
  295.5 4.0 fusion.217
  301.6 3.1 reduce-window.80
  313.1 2.6 fusion.219
  327.3 4.0 fusion.217
  333.4 3.1 reduce-window.80
  359.1 4.0 fusion.217
  365.1 3.1 reduce-window.80
  389.2 18.8 %reduce-scatter.2.cloned.1.call-done = f32[1024,64]{0,1:T(8,128)} async-done(((f32[1024,256]{0,1:T(8,128)}), f32[1024,64]{0,1:T(8,128)}) %reduce-scatter.2.cloned.1.call-update) | async-done | bytes 262160 | tf_op jit(solution)/shard_map/reduce_scatter | solution.py:170
  (337 shorter events, 174.3 us)
Async XLA Ops:
  7.2 238.8 %all-gather.4.cloned.1.call-start = ((), (), s32[]{:S(2)}) async-start(), calls=%async_computation.2 | async-start | bytes 2359296 | tf_op jit(solution)/shard_map/all_gather | solution.py:153
  16.6 46.7 %copy-start.12 = (f32[8,64,128]{2,1,0:T(8,128)}, f32[8,64,128]{2,1,0:T(8,128)S(1)}, u32[]{:S(2)}) copy-start(f32[8,64,128]{2,1,0:T(8,128)S(1)} %fusion.106) | copy-start | bytes 786436
  16.6 12.4 %collective-permute-start = (f32[1,8,64,128]{3,2,1,0:T(8,128)S(1)}, f32[1,8,64,128]{3,2,1,0:T(8,128)S(1)}, u32[]{:S(2)}, u32[]{:S(2)}) collective-permute-start(f32[1,8,64,128]{3,2,1,0:T(8,128)S(1)} %bitcast.375), channel_id=1, source_target_pairs={{0,1},{1,2},{2,3},{3,4},{4,5},{5,6},{6,7},{7,0},{8,9},{9,10},{10,1... | collective-permute-start | bytes 786440 | tf_op jit(solution)/shard_map/ppermute | solution.py:95
  29.0 34.3 %copy-start.14 = (f32[1,8,64,128]{3,2,1,0:T(8,128)}, f32[1,8,64,128]{3,2,1,0:T(8,128)S(1)}, u32[]{:S(2)}) copy-start(f32[1,8,64,128]{3,2,1,0:T(8,128)S(1)} %collective-permute-done) | copy-start | bytes 786436
  29.0 10.9 %collective-permute-start.1 = (f32[1,8,64,128]{3,2,1,0:T(8,128)S(1)}, f32[1,8,64,128]{3,2,1,0:T(8,128)S(1)}, u32[]{:S(2)}, u32[]{:S(2)}) collective-permute-start(f32[1,8,64,128]{3,2,1,0:T(8,128)S(1)} %collective-permute-done), channel_id=1, source_target_pairs={{0,1},{1,2},{2,3},{3,4},{4,5},{5,6},{6,7},{7,0},{8,9},{9,10},{10,1... | collective-permute-start | bytes 786440 | tf_op jit(solution)/shard_map/ppermute | solution.py:95
  29.0 32.2 %collective-permute-start.4 = (f32[1,8,64,128]{3,2,1,0:T(8,128)S(1)}, f32[1,8,64,128]{3,2,1,0:T(8,128)}, u32[]{:S(2)}, u32[]{:S(2)}) collective-permute-start(f32[1,8,64,128]{3,2,1,0:T(8,128)S(1)} %bitcast.376), channel_id=1, source_target_pairs={{1,0},{2,1},{3,2},{4,3},{5,4},{6,5},{7,6},{0,7},{9,8},{10,9},{11,1... | collective-permute-start | bytes 786440 | tf_op jit(solution)/shard_map/ppermute | solution.py:100
  39.9 23.4 %copy-start.16 = (f32[1,8,64,128]{3,2,1,0:T(8,128)}, f32[1,8,64,128]{3,2,1,0:T(8,128)S(1)}, u32[]{:S(2)}) copy-start(f32[1,8,64,128]{3,2,1,0:T(8,128)S(1)} %collective-permute-done.1) | copy-start | bytes 786436
  39.9 21.6 %collective-permute-start.2 = (f32[1,8,64,128]{3,2,1,0:T(8,128)S(1)}, f32[1,8,64,128]{3,2,1,0:T(8,128)}, u32[]{:S(2)}, u32[]{:S(2)}) collective-permute-start(f32[1,8,64,128]{3,2,1,0:T(8,128)S(1)} %collective-permute-done.1), channel_id=1, source_target_pairs={{0,1},{1,2},{2,3},{3,4},{4,5},{5,6},{6,7},{7,0},{8,9},{9,10},{10,1... | collective-permute-start | bytes 786440 | tf_op jit(solution)/shard_map/ppermute | solution.py:95
  61.1 9.5 %collective-permute-start.5 = (f32[1,8,64,128]{3,2,1,0:T(8,128)}, f32[1,8,64,128]{3,2,1,0:T(8,128)}, u32[]{:S(2)}, u32[]{:S(2)}) collective-permute-start(f32[1,8,64,128]{3,2,1,0:T(8,128)} %collective-permute-done.4), channel_id=1, source_target_pairs={{1,0},{2,1},{3,2},{4,3},{5,4},{6,5},{7,6},{0,7},{9,8},{10,9},{11,1... | collective-permute-start | bytes 786440 | tf_op jit(solution)/shard_map/ppermute | solution.py:100
  61.5 12.2 %collective-permute-start.3 = (f32[1,8,64,128]{3,2,1,0:T(8,128)}, f32[1,8,64,128]{3,2,1,0:T(8,128)}, u32[]{:S(2)}, u32[]{:S(2)}) collective-permute-start(f32[1,8,64,128]{3,2,1,0:T(8,128)} %collective-permute-done.2), channel_id=1, source_target_pairs={{0,1},{1,2},{2,3},{3,4},{4,5},{5,6},{6,7},{7,0},{8,9},{9,10},{10,1... | collective-permute-start | bytes 786440 | tf_op jit(solution)/shard_map/ppermute | solution.py:95
  68.0 117.6 %copy-start.1 = (bf16[1024,512]{0,1:T(8,128)(2,1)}, bf16[1024,512]{0,1:T(8,128)(2,1)S(1)}, u32[]{:S(2)}) copy-start(bf16[1024,512]{0,1:T(8,128)(2,1)S(1)} %copy.69) | copy-start | bytes 3145732
  68.0 9.0 %copy-start.17 = (f32[1,8,64,128]{3,2,1,0:T(8,128)S(1)}, f32[1,8,64,128]{3,2,1,0:T(8,128)}, u32[]{:S(2)}) copy-start(f32[1,8,64,128]{3,2,1,0:T(8,128)} %copy-done.16) | copy-start | bytes 786436
  68.0 9.7 %copy-start.15 = (f32[1,8,64,128]{3,2,1,0:T(8,128)S(1)}, f32[1,8,64,128]{3,2,1,0:T(8,128)}, u32[]{:S(2)}) copy-start(f32[1,8,64,128]{3,2,1,0:T(8,128)} %copy-done.14) | copy-start | bytes 786436
  68.0 10.4 %copy-start.13 = (f32[8,64,128]{2,1,0:T(8,128)S(1)}, f32[8,64,128]{2,1,0:T(8,128)}, u32[]{:S(2)}) copy-start(f32[8,64,128]{2,1,0:T(8,128)} %copy-done.12) | copy-start | bytes 786436
  69.9 115.6 %copy-start.2 = (bf16[1024,512]{0,1:T(8,128)(2,1)}, bf16[1024,512]{0,1:T(8,128)(2,1)S(1)}, u32[]{:S(2)}) copy-start(bf16[1024,512]{0,1:T(8,128)(2,1)S(1)} %copy.73) | copy-start | bytes 3145732
  70.7 11.9 %collective-permute-start.6 = (f32[1,8,64,128]{3,2,1,0:T(8,128)}, f32[1,8,64,128]{3,2,1,0:T(8,128)S(1)}, u32[]{:S(2)}, u32[]{:S(2)}) collective-permute-start(f32[1,8,64,128]{3,2,1,0:T(8,128)} %collective-permute-done.5), channel_id=1, source_target_pairs={{1,0},{2,1},{3,2},{4,3},{5,4},{6,5},{7,6},{0,7},{9,8},{10,9},{11,1... | collective-permute-start | bytes 786440 | tf_op jit(solution)/shard_map/ppermute | solution.py:100
  86.9 4.4 %copy-start.7 = (f32[1024,8]{0,1:T(8,128)S(1)}, f32[1024,8]{0,1:T(8,128)}, u32[]{:S(2)}) copy-start(f32[1024,8]{0,1:T(8,128)} %param.17) | copy-start | bytes 98308
  192.8 4.6 %copy-start.11 = (bf16[1024,128]{1,0:T(8,128)(2,1)S(1)}, bf16[1024,128]{1,0:T(8,128)(2,1)}, u32[]{:S(2)}) copy-start(bf16[1024,128]{1,0:T(8,128)(2,1)} %param.16) | copy-start | bytes 786436
  199.3 208.8 %reduce-scatter.2.cloned.1.call-start = ((), (), s32[]{:S(2)}) async-start(), calls=%async_computation.1 | async-start | bytes 1310720 | tf_op jit(solution)/shard_map/reduce_scatter | solution.py:170
  263.7 4.0 copy-start.20
  274.9 6.4 %copy-start.4 = (bf16[4,256,8,64]{1,3,2,0:T(8,128)(2,1)S(1)}, bf16[4,256,8,64]{1,3,2,0:T(8,128)(2,1)}, u32[]{:S(2)}) copy-start(bf16[4,256,8,64]{1,3,2,0:T(8,128)(2,1)} %get-tuple-element.873) | copy-start | bytes 3145732 | tf_op jit(solution)/shard_map/transpose(jvp())/while
  274.9 6.4 %copy-start.21 = (f32[256,8]{0,1:T(8,128)S(1)}, f32[256,8]{0,1:T(8,128)}, u32[]{:S(2)}) copy-start(f32[256,8]{0,1:T(8,128)} %copy-done.20) | copy-start | bytes 24580 | tf_op jit(solution)/shard_map/transpose(jvp())/while
  295.5 4.0 copy-start.20
  306.7 6.5 %copy-start.4 = (bf16[4,256,8,64]{1,3,2,0:T(8,128)(2,1)S(1)}, bf16[4,256,8,64]{1,3,2,0:T(8,128)(2,1)}, u32[]{:S(2)}) copy-start(bf16[4,256,8,64]{1,3,2,0:T(8,128)(2,1)} %get-tuple-element.873) | copy-start | bytes 3145732 | tf_op jit(solution)/shard_map/transpose(jvp())/while
  306.7 6.5 %copy-start.21 = (f32[256,8]{0,1:T(8,128)S(1)}, f32[256,8]{0,1:T(8,128)}, u32[]{:S(2)}) copy-start(f32[256,8]{0,1:T(8,128)} %copy-done.20) | copy-start | bytes 24580 | tf_op jit(solution)/shard_map/transpose(jvp())/while
  327.3 4.0 copy-start.20
  338.5 6.4 %copy-start.4 = (bf16[4,256,8,64]{1,3,2,0:T(8,128)(2,1)S(1)}, bf16[4,256,8,64]{1,3,2,0:T(8,128)(2,1)}, u32[]{:S(2)}) copy-start(bf16[4,256,8,64]{1,3,2,0:T(8,128)(2,1)} %get-tuple-element.873) | copy-start | bytes 3145732 | tf_op jit(solution)/shard_map/transpose(jvp())/while
  338.5 6.4 %copy-start.21 = (f32[256,8]{0,1:T(8,128)S(1)}, f32[256,8]{0,1:T(8,128)}, u32[]{:S(2)}) copy-start(f32[256,8]{0,1:T(8,128)} %copy-done.20) | copy-start | bytes 24580 | tf_op jit(solution)/shard_map/transpose(jvp())/while
  344.9 3.6 copy-start.19
  359.1 4.0 copy-start.20
  370.2 6.4 %copy-start.4 = (bf16[4,256,8,64]{1,3,2,0:T(8,128)(2,1)S(1)}, bf16[4,256,8,64]{1,3,2,0:T(8,128)(2,1)}, u32[]{:S(2)}) copy-start(bf16[4,256,8,64]{1,3,2,0:T(8,128)(2,1)} %get-tuple-element.873) | copy-start | bytes 3145732 | tf_op jit(solution)/shard_map/transpose(jvp())/while
  370.2 6.4 %copy-start.21 = (f32[256,8]{0,1:T(8,128)S(1)}, f32[256,8]{0,1:T(8,128)}, u32[]{:S(2)}) copy-start(f32[256,8]{0,1:T(8,128)} %copy-done.20) | copy-start | bytes 24580 | tf_op jit(solution)/shard_map/transpose(jvp())/while
  (18 other events, 27.9 us)
Sparse Core Ops, SparseCore 0:
  199.4 46.5 all-gather.3
  384.7 23.2 reduce-scatter.1
